TPU v7x, 128 devices: a whole 4x4x4 slice. The times are simulated.
128 devices in a mesh: ep: 4 (over x), tm: 32 (over y, z, core).
Axes of the slice: x: 4, y: 4, z: 4, core: 2. Of those that a mesh axis runs over, the one named last changes fastest.
Arguments:
- predictions: float32 [128, 1048576], P('ep', 'tm'), may hold values from -6 to 6
- leaf_index: int32 [128, 1048576], P('ep', 'tm'), may hold values from 0 to 63
- events: int32 [128, 1048576], P('ep', 'tm'), may hold values 0 or 1
- tie_start: int32 [1048576], P('tm'), may hold values from 0 to 1, as said below
Outputs:
- new_pred: float32 [128, 1048576], P('ep', 'tm')
- leaf_weights: float32 [128, 64], P('ep')
- grad_hess: bfloat16 [2, 128, 32, 32768], P(None, None, 'tm', 'ep')
Inputs may be any that keep to these rules, and one draw needn't show every extreme that they name: `tie_start`: every row whose index is a multiple of 128 begins a tie group.
All inputs are finite; a program needn't handle non-finite values. No bound on the sum of `events` on one device may be relied on, other than what follows from the above.
Results may differ from a plain program's by a relative error of at most 0.0023.
Values may be sent and summed in bfloat16 or wider, within the bound.
A program may use at most 128 MiB of HBM per device.

v0:
```python
import math
import jax
import jax.numpy as jnp
from jax import lax
from jax.sharding import PartitionSpec as P

LEAVES = 64


def prefix(part, axis, combine, identity, reverse):
    count = lax.axis_size(axis)
    place = lax.axis_index(axis)
    ahead = count - 1 - place if reverse else place
    gathered = jax.tree.map(lambda a: lax.all_gather(a, axis), part)
    state = jax.tree.map(lambda a, e: jnp.zeros_like(a) + jnp.asarray(e, a.dtype), part, identity)

    def one(turn, state):
        source = count - 1 - turn if reverse else turn
        return combine(
            state, jax.tree.map(lambda a: lax.dynamic_index_in_dim(a, source, 0, False), gathered)
        )

    return lax.fori_loop(0, ahead, one, state)


def tile_matrices(tie_start):
    length = tie_start.shape[0]
    blocks = length // 128
    starts = tie_start.reshape(blocks, 128)
    labels = jnp.arange(128, dtype=jnp.int32)
    first_local = lax.cummax(jnp.where(starts == 1, labels[None, :], 0), axis=1)
    next_start = jnp.concatenate([starts[:, 1:], jnp.ones((blocks, 1), jnp.int32)], axis=1)
    last_local = lax.cummin(jnp.where(next_start == 1, labels[None, :], 127), axis=1, reverse=True)
    backward = (labels[None, :, None] >= first_local[:, None, :]).astype(jnp.float32)
    forward = (labels[None, :, None] <= last_local[:, None, :]).astype(jnp.float32)
    return (backward, forward)


def block_cumsum(values, matrices, from_end):
    groups = values.shape[0]
    length = values.shape[1]
    blocks = length // 128
    shaped = values.reshape(groups, blocks, 128)
    within = jnp.einsum("ebj,bji->ebi", shaped, matrices, precision=lax.Precision.HIGHEST)
    totals = jnp.sum(shaped, axis=2)
    if from_end:
        offsets = jnp.cumsum(totals[:, ::-1], axis=1)[:, ::-1] - totals
    else:
        offsets = jnp.cumsum(totals, axis=1) - totals
    return (within + offsets[:, :, None]).reshape(groups, length)


def add_values(earlier, later):
    return jax.tree.map(lambda left, right: left + right, earlier, later)


def leaf_partials(leaf_index, gradient, hessian, leaves):
    length = leaf_index.shape[1]
    width = math.gcd(length, 2048)
    labels = jnp.arange(leaves, dtype=jnp.int32)

    def one_block(step, totals):
        start = step * width
        part_leaf = lax.dynamic_slice_in_dim(leaf_index, start, width, 1)
        part_grad = lax.dynamic_slice_in_dim(gradient, start, width, 1)
        part_hess = lax.dynamic_slice_in_dim(hessian, start, width, 1)
        hits = part_leaf[:, None, :] == labels[None, :, None]
        gsum = jnp.sum(jnp.where(hits, part_grad[:, None, :], 0.0), axis=2)
        hsum = jnp.sum(jnp.where(hits, part_hess[:, None, :], 0.0), axis=2)
        return totals + jnp.stack([gsum, hsum], axis=1)

    empty = jnp.zeros((leaf_index.shape[0], 2, leaves), jnp.float32)
    return lax.fori_loop(0, length // width, one_block, empty)


def leaf_lookup(leaf_index, table):
    length = leaf_index.shape[1]
    width = math.gcd(length, 2048)
    labels = jnp.arange(table.shape[1], dtype=jnp.int32)

    def one_block(step, result):
        start = step * width
        part_leaf = lax.dynamic_slice_in_dim(leaf_index, start, width, 1)
        hits = part_leaf[:, None, :] == labels[None, :, None]
        picked = jnp.sum(jnp.where(hits, table[:, :, None], 0.0), axis=1)
        return lax.dynamic_update_slice_in_dim(result, picked, start, 1)

    empty = jnp.zeros(leaf_index.shape, jnp.float32)
    return lax.fori_loop(0, length // width, one_block, empty)


def on_device(predictions, leaf_index, events, tie_start):
    groups = predictions.shape[0]
    length = predictions.shape[1]
    backward, forward = tile_matrices(tie_start)
    weight = jnp.exp(predictions)
    local_risk = block_cumsum(weight, backward, True)
    block_total = local_risk[:, 0]
    zero_column = jnp.zeros((groups,), jnp.float32)
    later_total = prefix(block_total, "tm", add_values, zero_column, True)
    risk = local_risk + later_total[:, None]
    observed = events.astype(jnp.float32)
    inv_one = observed / risk
    inv_two = inv_one / risk
    local_one = block_cumsum(inv_one, forward, False)
    local_two = block_cumsum(inv_two, forward, False)
    totals_pair = (local_one[:, -1], local_two[:, -1])
    earlier_one, earlier_two = prefix(
        totals_pair, "tm", add_values, (zero_column, zero_column), False
    )
    accum_one = local_one + earlier_one[:, None]
    accum_two = local_two + earlier_two[:, None]
    gradient = weight * accum_one - observed
    hessian = weight * accum_one - weight * weight * accum_two
    stacked = jnp.stack([gradient, hessian]).astype(jnp.bfloat16).reshape(2, groups, 1, length)
    grad_hess = lax.all_to_all(stacked, "ep", split_axis=3, concat_axis=1, tiled=True)
    partial_value = leaf_partials(leaf_index, gradient, hessian, LEAVES)
    totals = lax.psum(partial_value, "tm")
    leaf_weights = -totals[:, 0] / (totals[:, 1] + 1.0)
    new_pred = predictions + leaf_lookup(leaf_index, leaf_weights)
    return (new_pred, leaf_weights, grad_hess)


def solution(mesh):
    placed = (P("ep", "tm"), P("ep", "tm"), P("ep", "tm"), P("tm"))
    return jax.shard_map(
        on_device,
        mesh=mesh,
        in_specs=placed,
        out_specs=(P("ep", "tm"), P("ep", None), P(None, None, "tm", "ep")),
        check_vma=False,
    )
```

profile of v0, /device:TPU:2, one launch (start us, length us, event | category | flops | bytes accessed | tf_op | source)
XLA Modules:
  0.0 666.5 jit_solution(1025747727024494581)
XLA Ops:
  0.6 6.2 exponential_bitcast_fusion.1
  12.6 10.0 %fusion.22 = f32[256,4,8,128]{3,2,1,0:T(8,128)S(1)} fusion(f32[4,256,8,128]{3,2,1,0:T(8,128)} %get-tuple-element.397, s32[256,128]{1,0:T(8,128)S(1)} %copy.130, f32[32,256]{0,1:T(8,128)S(1)} %copy.134), kind=kOutput, calls=%fused_computation.44 | convolution fusion | flops 1615855616 | bytes 8552448 | tf_op jit(solution)/shard_map/ebj,bji->ebi/dot_general | solution.py:44
  26.2 68.6 %all-reduce.1 = f32[1024]{0:T(1024)S(1)} all-reduce(f32[1024]{0:T(1024)S(1)} %dynamic-update-slice), channel_id=2, replica_groups=mesh['ep'=4,'tm'=32] {'tm'}, use_global_device_ids=true, to_apply=%add.1 | all-reduce | flops 1024 | bytes 8192
  96.5 4.4 reduce_window_min.10
  101.0 9.3 %fusion.34 = (f32[4,8,256,128]{3,1,2,0:T(8,128)}, f32[4,256,8,128]{3,2,1,0:T(8,128)}, f32[4,256,8,128]{3,2,1,0:T(8,128)}, f32[4,8,256,128]{3,1,2,0:T(8,128)S(1)}) fusion(f32[32]{0:T(128)S(1)} %get-tuple-element.296, f32[256,4,8,128]{3,2,1,0:T(8,128)} %copy-done.1, s32[32,32768]{1,0:T(8,128)} %param.14), kind=kLoop, calls=%fused_computation.79 | loop fusion | flops 5242880 | bytes 25165952
  113.4 10.0 %fusion.21 = f32[256,4,8,128]{3,2,1,0:T(8,128)S(1)} fusion(f32[4,256,8,128]{3,2,1,0:T(8,128)} %get-tuple-element.394, s32[256,128]{1,0:T(8,128)S(1)} %copy.128, f32[32,256]{0,1:T(8,128)S(1)} %copy.139), kind=kOutput, calls=%fused_computation.42 | convolution fusion | flops 1615855616 | bytes 8552448 | tf_op jit(solution)/shard_map/ebj,bji->ebi/dot_general | solution.py:44
  130.0 10.0 %fusion.20 = f32[256,4,8,128]{3,2,1,0:T(8,128)S(1)} fusion(f32[4,256,8,128]{3,2,1,0:T(8,128)} %get-tuple-element.393, s32[256,128]{1,0:T(8,128)S(1)} %copy.128, f32[32,256]{0,1:T(8,128)S(1)} %copy.144), kind=kOutput, calls=%fused_computation.40 | convolution fusion | flops 1615855616 | bytes 8552448 | tf_op jit(solution)/shard_map/ebj,bji->ebi/dot_general | solution.py:44
  142.7 64.1 %all-reduce.4 = (f32[1024]{0:T(1024)S(1)}, f32[1024]{0:T(1024)S(1)}) all-reduce(f32[1024]{0:T(1024)S(1)} %dynamic-update-slice.1, f32[1024]{0:T(1024)S(1)} %dynamic-update-slice.2), channel_id=3, replica_groups=mesh['ep'=4,'tm'=32] {'tm'}, use_global_device_ids=true, to_apply=%add.2 | all-reduce | flops 2048 | bytes 16384
  206.9 10.2 %convert_bitcast_fusion = (bf16[1,32,1,32768]{3,1,2,0:T(8,128)(2,1)S(1)}, f32[32,32768]{1,0:T(8,128)}, bf16[1,32,1,32768]{3,1,2,0:T(8,128)(2,1)S(1)}, f32[32,32768]{1,0:T(8,128)}) fusion(f32[32]{0:T(128)S(1)} %get-tuple-element.298, f32[256,4,8,128]{3,2,1,0:T(8,128)} %copy-done.2, f32[32]{0:T(128)S(1)} %get-tuple-element.297, f32[256,4,8,128]{3,2,1,0:T(8,128)} %copy-done, ...), kind=kLoop, calls=%fused_computation.52 | loop fusion | flops 10485760 | bytes 29360384 | tf_op jit(solution)/shard_map/stack | solution.py:115
  219.5 33.0 %copy.146 = bf16[2,32,1,32768]{1,0,2,3:T(2,128)(2,1)} copy(bf16[2,32,1,32768]{3,1,2,0:T(8,128)(2,1)} %pad_maximum_fusion) | data formatting | bytes 8388608 | tf_op jit(solution)/shard_map/stack | solution.py:115
  252.5 19.2 %reshape.184 = bf16[4,2,262144]{2,1,0:T(2,128)(2,1)} reshape(bf16[32768,1,2,32]{3,2,1,0:T(2,128)(2,1)} %bitcast.143) | data formatting | bytes 8388608
  271.7 5.3 all-to-all-start
  277.1 117.7 %while.55 = (s32[]{:T(128)}, f32[32,2,64]{2,0,1:T(8,128)S(1)}, s32[32,32768]{1,0:T(8,128)}, f32[32,32768]{1,0:T(8,128)}, f32[32,32768]{1,0:T(8,128)}, /*index=5*/s32[]{:T(128)}, s32[]{:T(128)}, s32[]{:T(128)}, s32[]{:T(128)}) while((s32[]{:T(128)}, f32[32,2,64]{2,0,1:T(8,128)S(1)}, s32[32,32768]{1,0:T(8,128)}, ...), condition=%wide.region_18.19_spmd.clone, body=%wide.region_15.18_spmd.clone.sunk | while | flops 20979716 | bytes 2424997 | solution.py:73
  279.1 5.3 fusion.39
  286.5 5.3 fusion.39
  293.8 5.3 fusion.39
  301.2 5.3 fusion.39
  308.5 5.3 fusion.39
  315.9 5.3 fusion.39
  323.2 5.3 fusion.39
  330.6 5.3 fusion.39
  337.9 5.3 fusion.39
  345.3 5.3 fusion.39
  352.7 5.3 fusion.39
  360.0 5.3 fusion.39
  367.4 5.3 fusion.39
  374.7 5.3 fusion.39
  382.1 5.3 fusion.39
  389.4 5.3 fusion.39
  394.7 124.3 %psum.7 = f32[32,2,64]{2,0,1:T(8,128)S(1)} all-reduce(f32[32,2,64]{2,0,1:T(8,128)S(1)} %get-tuple-element.299), channel_id=1, replica_groups=mesh['ep'=4,'tm'=32] {'tm'}, use_global_device_ids=true, to_apply=%region_19.20 | all-reduce | flops 4096 | bytes 32768 | tf_op jit(solution)/shard_map/psum | solution.py:118
  521.3 80.5 %while.54 = (s32[]{:T(128)}, f32[32,32768]{1,0:T(8,128)}, s32[32,32768]{1,0:T(8,128)}, f32[32,64]{1,0:T(8,128)S(1)}, s32[]{:T(128)}, /*index=5*/s32[]{:T(128)}, s32[]{:T(128)}, s32[]{:T(128)}) while((s32[]{:T(128)}, f32[32,32768]{1,0:T(8,128)}, s32[32,32768]{1,0:T(8,128)}, f32[32,64]{1,0:T(8,128)S(1)}, s32[]{:T(128)}, ...), condition=%wide.region_22.23_spmd.clone, body=%wide.region_20.22_spmd.clone.sunk | while | flops 12517382 | bytes 1581203 | solution.py:89
  527.3 3.3 select_reduce_fusion.2
  532.4 3.3 select_reduce_fusion.2
  537.4 3.3 select_reduce_fusion.2
  542.4 3.3 select_reduce_fusion.2
  547.5 3.3 select_reduce_fusion.2
  552.5 3.3 select_reduce_fusion.2
  557.5 3.3 select_reduce_fusion.2
  562.6 3.3 select_reduce_fusion.2
  567.6 3.3 select_reduce_fusion.2
  572.6 3.3 select_reduce_fusion.2
  582.7 3.3 select_reduce_fusion.2
  587.7 3.3 select_reduce_fusion.2
  592.7 3.3 select_reduce_fusion.2
  601.8 5.9 add.165
  607.7 12.0 %reshape.185 = bf16[32768,1,2,32]{3,2,1,0:T(2,128)(2,1)} reshape(bf16[4,2,262144]{2,1,0:T(2,128)(2,1)} %all-to-all-done) | data formatting | bytes 8388608
  619.7 40.0 %copy.150 = bf16[2,32,1,4,8192]{4,3,1,0,2:T(4,128)(2,1)} copy(bf16[2,32,1,4,8192]{1,0,4,3,2:T(2,128)(2,1)} %bitcast.144) | data formatting | bytes 8388608 | tf_op jit(solution)/shard_map/all_to_all | solution.py:116
  659.8 6.5 copy.148
  (192 shorter events, 98.0 us)
Async XLA Ops:
  0.6 6.2 copy-start.5
  22.6 2.0 copy-start.1
  22.6 2.1 copy-start.6
  123.4 2.1 copy-start
  123.4 3.7 copy-start.3
  140.0 2.0 copy-start.2
  271.7 336.0 %all-to-all-start = ((bf16[4,2,262144]{2,1,0:T(2,128)(2,1)}), bf16[4,2,262144]{2,1,0:T(2,128)(2,1)}, u32[]{:S(2)}, u32[]{:S(2)}) async-start(bf16[4,2,262144]{2,1,0:T(2,128)(2,1)} %reshape.184), calls=%async_computation | async-start | bytes 8388608 | tf_op jit(solution)/shard_map/all_to_all | solution.py:116
  601.8 5.9 copy-start.4
where the time goes:
time: 677 us; the launch traced here: 666 us
  blocking collectives  257 us (38%)
  local copies, waits for them, and re-layouts  195 us (29%)
  other arithmetic  176 us (26%)
  matrix products  30 us (4%)
    unnamed x2, blocking collectives  133 us
    psum x1, blocking collectives, on_device(): totals = lax.psum(partial_value, 'tm')  124 us
    reduce_sum x16, other arithmetic, one_block(): gsum = jnp.sum(jnp.where(hits, part_grad[:, None, :], 0.0), axis=2)  84.3 us
    reduce_sum x16, other arithmetic, one_block(): picked = jnp.sum(jnp.where(hits, table[:, :, None], 0.0), axis=1)  53.2 us
    unnamed x27, local copies, waits for them, and re-layouts  49.8 us
    all_to_all x2, local copies, waits for them, and re-layouts, on_device(): lax.all_to_all(stacked, 'ep', split_axis=3, concat_axis=1, tiled=True)  46.5 us
    another operation x1, local copies, waits for them, and re-layouts, on_device(): jnp.stack([gradient, hessian]).astype(jnp.bfloat16)  33 us
    dynamic_slice x32, local copies, waits for them, and re-layouts, one_block(): part_leaf = lax.dynamic_slice_in_dim(leaf_index, start, width, 1)  31.1 us
  transfers between devices with their start and end apart: 1, of which 0 were waited for; matrix products, arithmetic and copies ran while one was open for 31% of the time, Pallas kernels for 0%

commit v1 on v0

--- a/solution.py
+++ b/solution.py
@@ -90,6 +90,14 @@
 
 
 def on_device(predictions, leaf_index, events, tie_start):
+
+    def knots_arrange(frame_in, named_axis="ep"):
+        last = lax.psum(1, named_axis)
+        x_now = jnp.split(frame_in, last, axis=3)
+        back = jnp.stack(x_now, axis=0)
+        next_value = lax.all_to_all(back, named_axis, 0, 0)
+        return jnp.concatenate(next_value, axis=1)
+
     groups = predictions.shape[0]
     length = predictions.shape[1]
     backward, forward = tile_matrices(tie_start)
@@ -113,7 +121,7 @@
     gradient = weight * accum_one - observed
     hessian = weight * accum_one - weight * weight * accum_two
     stacked = jnp.stack([gradient, hessian]).astype(jnp.bfloat16).reshape(2, groups, 1, length)
-    grad_hess = lax.all_to_all(stacked, "ep", split_axis=3, concat_axis=1, tiled=True)
+    grad_hess = knots_arrange(stacked)
     partial_value = leaf_partials(leaf_index, gradient, hessian, LEAVES)
     totals = lax.psum(partial_value, "tm")
     leaf_weights = -totals[:, 0] / (totals[:, 1] + 1.0)

time: 677 us -> 568 us (0.84)
  local copies, waits for them, and re-layouts: 195 us -> 85.1 us
    all_to_all x2 -> x0, local copies, waits for them, and re-layouts: 46.5 us -> none  [on_device(): lax.all_to_all(stacked, 'ep', split_axis=3, concat_axis=1, tiled=True)]
    unnamed x27 -> x25, local copies, waits for them, and re-layouts: 49.8 us -> 15 us
    another operation x8, local copies, waits for them, and re-layouts: 33.4 us -> 0.55 us  [the longest x1 33 us: on_device(): jnp.stack([gradient, hessian]).astype(jnp.bfloat16)]
  transfers between devices with their start and end apart: 1 -> 1, of which waited for: 0 -> 0; matrix products, arithmetic and copies ran while one was open for 31% -> 37% of each run, Pallas kernels for 0% -> 0%
where the time goes in v1:
time: 568 us; the launch traced here: 558 us
  blocking collectives  257 us (45%)
  other arithmetic  177 us (31%)
  local copies, waits for them, and re-layouts  85.1 us (15%)
  matrix products  30.1 us (5%)
    unnamed x2, blocking collectives  132 us
    psum x1, blocking collectives, on_device(): totals = lax.psum(partial_value, 'tm')  124 us
    reduce_sum x16, other arithmetic, one_block(): gsum = jnp.sum(jnp.where(hits, part_grad[:, None, :], 0.0), axis=2)  84.3 us
    reduce_sum x16, other arithmetic, one_block(): picked = jnp.sum(jnp.where(hits, table[:, :, None], 0.0), axis=1)  53.2 us
    dynamic_slice x32, local copies, waits for them, and re-layouts, one_block(): part_leaf = lax.dynamic_slice_in_dim(leaf_index, start, width, 1)  31.1 us
    dot_general x3, matrix products, block_cumsum(): jnp.einsum('ebj,bji->ebi', shaped, matrices, precision=lax.Precision.HIGH...  30.1 us
    dynamic_slice x16, local copies, waits for them, and re-layouts, one_block(): part_hess = lax.dynamic_slice_in_dim(hessian, start, width, 1)  17.1 us
    unnamed x25, local copies, waits for them, and re-layouts  15 us
  transfers between devices with their start and end apart: 1, of which 0 were waited for; matrix products, arithmetic and copies ran while one was open for 37% of the time, Pallas kernels for 0%

profile of v1, /device:TPU:2, one launch (start us, length us, event | category | flops | bytes accessed | tf_op | source)
XLA Modules:
  0.0 557.7 jit_solution(16512008324978466375)
XLA Ops:
  0.6 4.7 exponential_bitcast_fusion.1
  9.0 10.0 %fusion.23 = f32[256,4,8,128]{3,2,1,0:T(8,128)S(1)} fusion(f32[4,256,8,128]{3,2,1,0:T(8,128)} %get-tuple-element.397, s32[256,128]{1,0:T(8,128)S(1)} %copy.68, f32[32,256]{0,1:T(8,128)S(1)} %copy.72), kind=kOutput, calls=%fused_computation.48 | convolution fusion | flops 1615855616 | bytes 8552448 | tf_op jit(solution)/shard_map/ebj,bji->ebi/dot_general | solution.py:44
  22.6 68.6 %all-reduce.1 = f32[1024]{0:T(1024)S(1)} all-reduce(f32[1024]{0:T(1024)S(1)} %dynamic-update-slice), channel_id=2, replica_groups=mesh['ep'=4,'tm'=32] {'tm'}, use_global_device_ids=true, to_apply=%add.1 | all-reduce | flops 1024 | bytes 8192
  92.6 9.4 %fusion.37 = (f32[4,8,256,128]{3,1,2,0:T(8,128)S(1)}, f32[4,256,8,128]{3,2,1,0:T(8,128)}, f32[4,256,8,128]{3,2,1,0:T(8,128)}, f32[4,8,256,128]{3,1,2,0:T(8,128)}) fusion(f32[32]{0:T(128)S(1)} %get-tuple-element.296, f32[256,4,8,128]{3,2,1,0:T(8,128)} %copy-done.2, s32[32,32768]{1,0:T(8,128)} %param.14), kind=kLoop, calls=%fused_computation.88 | loop fusion | flops 5242880 | bytes 25165952
  105.6 4.4 reduce_window_min.10
  110.1 10.0 %fusion.21 = f32[256,4,8,128]{3,2,1,0:T(8,128)S(1)} fusion(f32[4,256,8,128]{3,2,1,0:T(8,128)} %get-tuple-element.390, s32[256,128]{1,0:T(8,128)S(1)} %copy.66, f32[32,256]{0,1:T(8,128)S(1)} %copy.82), kind=kOutput, calls=%fused_computation.44 | convolution fusion | flops 1615855616 | bytes 8552448 | tf_op jit(solution)/shard_map/ebj,bji->ebi/dot_general | solution.py:44
  126.7 10.2 %fusion.22 = f32[256,4,8,128]{3,2,1,0:T(8,128)S(1)} fusion(f32[4,256,8,128]{3,2,1,0:T(8,128)} %get-tuple-element.391, s32[256,128]{1,0:T(8,128)S(1)} %copy.66, f32[32,256]{0,1:T(8,128)S(1)} %copy.77), kind=kOutput, calls=%fused_computation.46 | convolution fusion | flops 1615855616 | bytes 8552448 | tf_op jit(solution)/shard_map/ebj,bji->ebi/dot_general | solution.py:44
  139.5 63.7 %all-reduce.4 = (f32[1024]{0:T(1024)S(1)}, f32[1024]{0:T(1024)S(1)}) all-reduce(f32[1024]{0:T(1024)S(1)} %dynamic-update-slice.1, f32[1024]{0:T(1024)S(1)} %dynamic-update-slice.2), channel_id=3, replica_groups=mesh['ep'=4,'tm'=32] {'tm'}, use_global_device_ids=true, to_apply=%add.2 | all-reduce | flops 2048 | bytes 16384
  203.4 10.3 %convert_bitcast_fusion = (bf16[1,32,1,32768]{3,1,2,0:T(8,128)(2,1)S(1)}, f32[32,32768]{1,0:T(8,128)}, bf16[1,32,1,32768]{3,1,2,0:T(8,128)(2,1)S(1)}, f32[32,32768]{1,0:T(8,128)}) fusion(f32[32]{0:T(128)S(1)} %get-tuple-element.298, f32[256,4,8,128]{3,2,1,0:T(8,128)} %copy-done, f32[32]{0:T(128)S(1)} %get-tuple-element.297, f32[256,4,8,128]{3,2,1,0:T(8,128)} %copy-done.1, ...), kind=kLoop, calls=%fused_computation.56 | loop fusion | flops 10485760 | bytes 29360384 | tf_op jit(solution)/shard_map/stack | solution.py:123
  216.6 5.6 all-to-all-start
  222.2 117.7 %while.55 = (s32[]{:T(128)}, f32[32,2,64]{2,0,1:T(8,128)S(1)}, s32[32,32768]{1,0:T(8,128)}, f32[32,32768]{1,0:T(8,128)}, f32[32,32768]{1,0:T(8,128)}, /*index=5*/s32[]{:T(128)}, s32[]{:T(128)}, s32[]{:T(128)}, s32[]{:T(128)}) while((s32[]{:T(128)}, f32[32,2,64]{2,0,1:T(8,128)S(1)}, s32[32,32768]{1,0:T(8,128)}, ...), condition=%wide.region_18.19_spmd.clone, body=%wide.region_15.18_spmd.clone.sunk | while | flops 20979716 | bytes 2424989 | solution.py:73
  224.2 5.3 fusion.42
  231.6 5.3 fusion.42
  238.9 5.3 fusion.42
  246.3 5.3 fusion.42
  253.7 5.3 fusion.42
  261.0 5.3 fusion.42
  268.4 5.3 fusion.42
  275.7 5.3 fusion.42
  283.1 5.3 fusion.42
  290.4 5.3 fusion.42
  297.8 5.3 fusion.42
  305.1 5.3 fusion.42
  312.5 5.3 fusion.42
  319.9 5.3 fusion.42
  327.2 5.3 fusion.42
  334.6 5.3 fusion.42
  339.9 124.3 %psum.7 = f32[32,2,64]{2,0,1:T(8,128)S(1)} all-reduce(f32[32,2,64]{2,0,1:T(8,128)S(1)} %get-tuple-element.299), channel_id=1, replica_groups=mesh['ep'=4,'tm'=32] {'tm'}, use_global_device_ids=true, to_apply=%region_19.20 | all-reduce | flops 4096 | bytes 32768 | tf_op jit(solution)/shard_map/psum | solution.py:126
  464.2 2.3 broadcast_in_dim.125
  466.5 80.5 %while.54 = (s32[]{:T(128)}, f32[32,32768]{1,0:T(8,128)}, s32[32,32768]{1,0:T(8,128)}, f32[32,64]{1,0:T(8,128)S(1)}, s32[]{:T(128)}, /*index=5*/s32[]{:T(128)}, s32[]{:T(128)}, s32[]{:T(128)}) while((s32[]{:T(128)}, f32[32,32768]{1,0:T(8,128)}, s32[32,32768]{1,0:T(8,128)}, f32[32,64]{1,0:T(8,128)S(1)}, s32[]{:T(128)}, ...), condition=%wide.region_22.23_spmd.clone, body=%wide.region_20.22_spmd.clone.sunk | while | flops 12517382 | bytes 1581195 | solution.py:89
  467.4 3.3 select_reduce_fusion.2
  472.5 3.3 select_reduce_fusion.2
  477.5 3.3 select_reduce_fusion.2
  482.5 3.3 select_reduce_fusion.2
  487.6 3.3 select_reduce_fusion.2
  492.6 3.3 select_reduce_fusion.2
  497.6 3.3 select_reduce_fusion.2
  502.6 3.3 select_reduce_fusion.2
  507.7 3.3 select_reduce_fusion.2
  512.7 3.3 select_reduce_fusion.2
  517.7 3.3 select_reduce_fusion.2
  522.8 3.3 select_reduce_fusion.2
  527.8 3.3 select_reduce_fusion.2
  532.8 3.3 select_reduce_fusion.2
  537.8 3.3 select_reduce_fusion.2
  542.9 3.3 select_reduce_fusion.2
  546.9 5.9 %add.165 = f32[32,32768]{1,0:T(8,128)} add(f32[32,32768]{1,0:T(8,128)} %param.12, f32[32,32768]{1,0:T(8,128)} %get-tuple-element.300) | non-fusion elementwise | flops 1048576 | bytes 12582912 | tf_op jit(solution)/shard_map/add | solution.py:128
  552.8 4.6 copy.87
  (191 shorter events, 84.3 us)
Async XLA Ops:
  6.1 2.5 copy-start.5
  19.0 2.0 copy-start.2
  19.0 2.1 copy-start.6
  120.1 2.1 copy-start
  120.1 3.7 copy-start.3
  136.9 2.0 copy-start.1
  216.6 336.2 %all-to-all-start = ((bf16[4,2,32,1,8192]{4,2,1,3,0:T(8,128)(2,1)}), bf16[4,2,32,1,8192]{4,2,1,3,0:T(8,128)(2,1)}, u32[]{:S(2)}, u32[]{:S(2)}) async-start(bf16[4,2,32,1,8192]{4,2,1,3,0:T(8,128)(2,1)} %pad_maximum_fusion.1), calls=%async_computation | async-start | bytes 8388608 | tf_op jit(solution)/shard_map/all_to_all | solution.py:98
  546.9 5.9 %copy-start.4 = (f32[32,64]{1,0:T(8,128)}, f32[32,64]{1,0:T(8,128)S(1)}, u32[]{:S(2)}) copy-start(f32[32,64]{1,0:T(8,128)S(1)} %get-tuple-element.635) | copy-start | bytes 24580
